TPU v7x, 256 devices: a whole 4x4x8 slice. The times are simulated.
256 devices in a mesh: sec: 16 (over x, y_hi, core), span: 16 (over z, y_lo).
Axes of the slice: x: 4, y: 4 (y_hi: 2, y_lo: 2; y = y_hi * 2 + y_lo), z: 8, core: 2. Of those that a mesh axis runs over, the one named last changes fastest.
Arguments:
- density: float32 [384, 4096], P('sec', 'span'), may hold values from 0.5 to 2
- fields: float32 [4, 384, 4096], P(None, 'sec', 'span'), may hold values from -6 to 6
- bins: int32 [384, 4096], P('sec', 'span'), may hold values from 0 to 127
- owner: int32 [384], P('sec'), may hold values from 0 to 255
- species: float32 [256, 32, 128], P(('sec', 'span')), may hold values from -6 to 6
- rate_matrix: float32 [32, 32], replicated, may hold values from -1 to 1
- inv_weight: float32 [32], replicated, may hold values from 0.5 to 2
- formation: float32 [32], replicated, may hold values from -4 to 4
Outputs:
- species_out: float32 [256, 32, 128], P(('sec', 'span'))
- density_out: float32 [384, 4096], P('sec', 'span')
- fields_out: float32 [4, 384, 4096], P(None, 'sec', 'span')
All inputs are finite; a program needn't handle non-finite values.
Results may differ from a plain program's by a relative error of at most 0.0003.
Values sent between devices are 32-bit elements; how exact they have to be, the bound alone decides.
No kernel may reach another device: no remote copies, remote signals or barrier semaphores. Data moves between devices by JAX's collectives and lax.ppermute only.
A program may use at most 64 MiB of HBM per device.

v0:
```python
import math
import jax
import jax.numpy as jnp
from jax import lax
from jax.sharding import PartitionSpec as P

COUPLING = 2


def from_behind(value, axis, steps):
    count = lax.axis_size(axis)
    first, last = (max(0, -steps), min(count, count - steps))
    return lax.ppermute(value, axis, [(source, source + steps) for source in range(first, last)])


def extended_2(shard, sides, width):
    for axis, dim in sides:
        count, length = (lax.axis_size(axis), shard.shape[dim])
        up = [(i, (i + 1) % count) for i in range(count)]
        down = [(j, i) for i, j in up]
        last = lax.slice_in_dim(shard, length - width, length, axis=dim)
        first = lax.slice_in_dim(shard, 0, width, axis=dim)
        before = lax.ppermute(last, axis, up)
        after = lax.ppermute(first, axis, down)
        shard = jnp.concatenate([before, shard, after], axis=dim)
    return shard


def column_sums(values, bins, nbins):
    cols, quant, zlen = values.shape
    block = math.gcd(cols, 16)
    value_blocks = values.reshape(cols // block, block, quant, zlen)
    bin_blocks = bins.reshape(cols // block, block, zlen)

    def one_block(pair):
        vals, labels = pair
        hot = (labels[:, :, None] == jnp.arange(nbins, dtype=jnp.int32)).astype(jnp.float32)
        return jnp.einsum("cqz,czb->cqb", vals, hot, precision=lax.Precision.HIGHEST)

    out = lax.map(one_block, (value_blocks, bin_blocks))
    return out.reshape(cols, quant * nbins)


def body(density, fields, bins, owner, species, rate_matrix, inv_weight, formation):
    nbins = species.shape[2]
    nspec = species.shape[1]
    sections = lax.axis_size("sec") * lax.axis_size("span")
    mine = lax.axis_index("sec") * lax.axis_size("span") + lax.axis_index("span")
    eta = (jnp.arange(nbins, dtype=jnp.float32) + 0.5) / nbins
    index = owner[:, None] * nbins + bins
    for step in range(COUPLING):
        values = jnp.stack([density] + [density * fields[k] for k in range(4)], axis=1)
        hist = column_sums(values, bins, nbins)
        hot = (owner[:, None] == jnp.arange(sections, dtype=jnp.int32)[None, :]).astype(jnp.float32)
        total = lax.psum(
            lax.dot_general(
                hot,
                hist,
                (((0,), (0,)), ((), ())),
                precision=lax.Precision.HIGHEST,
                preferred_element_type=jnp.float32,
            ),
            ("sec", "span"),
        )
        own = lax.dynamic_slice_in_dim(total, mine, 1, 0)
        own = own.reshape(5, nbins)
        weight = jnp.maximum(own[0], 1.0)
        cond = own[1:] / weight[None]
        current = species[0]
        before = from_behind(species, ("sec", "span"), 1)[0]
        temp = 1.0 + 4.0 * eta * (1.0 - eta) + 0.5 * jnp.tanh(cond[2])
        rate = jnp.exp(2.0 * (1.0 - 1.0 / temp))
        react = (
            jnp.dot(
                rate_matrix,
                current,
                precision=lax.Precision.HIGHEST,
                preferred_element_type=jnp.float32,
            )
            * rate[None, :]
        )
        padded = jnp.pad(current, ((0, 0), (1, 1)))
        lap = padded[:, 2:] + padded[:, :-2] - 2.0 * current
        mixing = 0.2 * jax.nn.sigmoid(cond[1])
        carried = 0.3 * jax.nn.sigmoid(cond[0])
        updated = (
            current + mixing[None, :] * lap - carried[None, :] * (current - before) + 0.2 * react
        )
        species = updated[None]
        mix = 1.0 + jnp.sum(inv_weight[:, None] * updated * updated, axis=0) / nspec
        rho_c = 1.0 / (temp * mix)
        temp_c = (
            temp
            + 0.1 * jnp.sum(formation[:, None] * react, axis=0)
            - 0.2 * jax.nn.sigmoid(cond[3]) * (temp - 0.5)
        )
        table = jnp.stack([rho_c, temp_c])[None]
        whole = lax.all_gather(table, ("sec", "span"), axis=0, tiled=True)
        rho_cell = whole[:, 0, :].reshape(-1)[index]
        temp_cell = whole[:, 1, :].reshape(-1)[index]
        extended = extended_2(fields, (("span", 2),), 1)
        lapz = extended[:, :, 2:] + extended[:, :, :-2] - 2.0 * fields
        fields = fields + 0.2 * lapz
        fields = fields.at[2].add(0.3 * (temp_cell - fields[2]))
        density = rho_cell
    return (species, density, fields)


def solution(mesh):
    return jax.shard_map(
        body,
        mesh=mesh,
        in_specs=(
            P("sec", "span"),
            P(None, "sec", "span"),
            P("sec", "span"),
            P("sec"),
            P(("sec", "span"), None, None),
            P(),
            P(),
            P(),
        ),
        out_specs=(P(("sec", "span"), None, None), P("sec", "span"), P(None, "sec", "span")),
        check_vma=False,
    )
```

profile of v0, /device:TPU:0, one launch (start us, length us, event | category | flops | bytes accessed | tf_op | source)
XLA Modules:
  0.0 1920.2 jit_solution(5151774485042406274)
XLA Ops:
  7.2 0.8 stack.38
  8.1 0.8 bitcast_multiply_fusion
  9.2 0.7 copy-done.2
  10.0 2.4 while.22
  10.0 0.8 fusion.68
  10.8 0.8 fusion.68
  11.6 0.8 fusion.68
  13.1 1.4 fusion.21
  15.2 1.8 collective-permute-start
  17.0 5.3 collective-permute-start.1
  22.5 1.6 collective-permute-done.1
  24.1 4.4 collective-permute-done.2
  28.7 242.0 %all-reduce.5.cloned.1.call-done = f32[256,640]{1,0:T(8,128)} async-done(((f32[256,640]{1,0:T(8,128)}), f32[256,640]{1,0:T(8,128)}) %all-reduce.5.cloned.1.call-update) | async-done | bytes 655376 | tf_op jit(solution)/shard_map/psum | solution.py:55
  270.7 0.7 fusion.46
  271.4 0.8 dynamic-slice.16
  273.1 624.5 %all-gather.2 = f32[256,2,128]{2,1,0:T(2,128)S(1)} all-gather(f32[1,2,128]{2,1,0:T(2,128)S(1)} %maximum_bitcast_fusion), channel_id=2, replica_groups=mesh['sec'=16,'span'=16] {'sec','span'}, dimensions={0}, use_global_device_ids=true | all-gather | bytes 263168 | tf_op jit(solution)/shard_map/all_gather | solution.py:98
  897.8 34.3 %gather_fusion.1 = f32[6144]{0:T(1024)S(1)} fusion(f32[32768]{0:T(1024)S(1)} %bitcast.132, s32[6144]{0:T(1024)S(1)} %broadcast_clamp_fusion), kind=kCustom, calls=%fused_computation.1 | custom fusion | bytes 73728 | tf_op jit(solution)/shard_map/gather | solution.py:100
  932.1 34.3 %gather_fusion = f32[6144]{0:T(1024)S(1)} fusion(f32[32768]{0:T(1024)S(1)} %bitcast.130, s32[6144]{0:T(1024)S(1)} %broadcast_clamp_fusion), kind=kCustom, calls=%fused_computation | custom fusion | bytes 73728 | tf_op jit(solution)/shard_map/gather | solution.py:99
  966.7 2.5 while.23
  966.7 0.8 fusion.70
  967.6 0.8 fusion.70
  968.4 0.8 fusion.70
  969.2 1.4 fusion.18
  970.8 2.0 collective-permute-start.5
  972.8 1.9 collective-permute-start.3
  975.0 2.1 collective-permute-done.5
  977.2 239.2 %all-reduce.7.cloned.1.call-done = f32[256,640]{1,0:T(8,128)} async-done(((f32[256,640]{1,0:T(8,128)}), f32[256,640]{1,0:T(8,128)}) %all-reduce.7.cloned.1.call-update) | async-done | bytes 655376 | tf_op jit(solution)/shard_map/psum | solution.py:55
  1217.0 0.8 dynamic-slice.18
  1218.0 0.7 fusion.26
  1218.8 624.5 %all-gather.3 = f32[256,2,128]{2,1,0:T(2,128)S(1)} all-gather(f32[1,2,128]{2,1,0:T(2,128)S(1)} %maximum_bitcast_fusion.1), channel_id=3, replica_groups=mesh['sec'=16,'span'=16] {'sec','span'}, dimensions={0}, use_global_device_ids=true | all-gather | bytes 263168 | tf_op jit(solution)/shard_map/all_gather | solution.py:98
  1843.5 34.3 %gather_fusion.3 = f32[6144]{0:T(1024)S(1)} fusion(f32[32768]{0:T(1024)S(1)} %bitcast.133, s32[6144]{0:T(1024)S(1)} %broadcast_clamp_fusion), kind=kCustom, calls=%fused_computation.3 | custom fusion | bytes 73728 | tf_op jit(solution)/shard_map/gather | solution.py:100
  1877.8 34.3 %gather_fusion.2 = f32[6144]{0:T(1024)S(1)} fusion(f32[32768]{0:T(1024)S(1)} %bitcast.131, s32[6144]{0:T(1024)S(1)} %broadcast_clamp_fusion), kind=kCustom, calls=%fused_computation.2 | custom fusion | bytes 73728 | tf_op jit(solution)/shard_map/gather | solution.py:99
  (68 shorter events, 6.4 us)
Async XLA Ops:
  7.2 265.1 %copy-start = (f32[32,32]{1,0:T(8,128)S(1)}, f32[32,32]{1,0:T(8,128)}, u32[]{:S(2)}) copy-start(f32[32,32]{1,0:T(8,128)} %param.21) | copy-start | bytes 12292
  7.2 263.5 %all-reduce.5.cloned.1.call-start = ((), (), s32[]{:S(2)}) async-start(), calls=%async_computation | async-start | bytes 1310720 | tf_op jit(solution)/shard_map/psum | solution.py:55
  7.2 0.8 copy-start.4
  9.2 0.7 copy-start.2
  12.4 0.7 copy-start.5
  14.5 0.7 copy-start.7
  14.5 2.5 copy-start.1
  14.5 1201.9 %all-reduce.7.cloned.1.call-start = ((), (), s32[]{:S(2)}) async-start(), calls=%async_computation.1 | async-start | bytes 1310720 | tf_op jit(solution)/shard_map/psum | solution.py:55
  15.2 257.0 %collective-permute-start = (f32[1,32,128]{2,1,0:T(8,128)S(1)}, f32[1,32,128]{2,1,0:T(8,128)S(1)}, u32[]{:S(2)}, u32[]{:S(2)}) collective-permute-start(f32[1,32,128]{2,1,0:T(8,128)S(1)} %copy-done.7), channel_id=1, source_target_pairs={{0,1},{1,2},{2,3},{3,4},{4,5},{5,6},{6,7},{7,8},{8,9},{9,10},{10,1... | collective-permute-start | bytes 49160 | tf_op jit(solution)/shard_map/ppermute | solution.py:13
  17.0 7.1 collective-permute-start.1
  22.4 6.2 collective-permute-start.2
  272.2 0.7 copy-start.6
  272.2 0.7 copy-start.8
  970.7 4.2 collective-permute-start.4
  970.8 6.3 collective-permute-start.5
  972.8 245.3 %collective-permute-start.3 = (f32[1,32,128]{2,1,0:T(8,128)S(1)}, f32[1,32,128]{2,1,0:T(8,128)S(1)}, u32[]{:S(2)}, u32[]{:S(2)}) collective-permute-start(f32[1,32,128]{2,1,0:T(8,128)S(1)} %bitcast.139), channel_id=1, source_target_pairs={{0,1},{1,2},{2,3},{3,4},{4,5},{5,6},{6,7},{7,8},{8,9},{9,10},{10,1... | collective-permute-start | bytes 49160 | tf_op jit(solution)/shard_map/ppermute | solution.py:13
  1912.7 0.6 copy-start.3
Sparse Core Ops, SparseCore 0:
  14.6 256.0 all-reduce.4
  970.8 245.5 all-reduce.6
where the time goes:
time: 1920 us
  blocking collectives  1250 us (65%)
  waiting for transfers between devices  490 us (26%)
  local copies, waits for them, and re-layouts  145 us (8%)
    all_gather x2, blocking collectives, body(): whole = lax.all_gather(table, ('sec', 'span'), axis=0, tiled=True)  1250 us
    psum x2, waiting for transfers between devices, body(): lax.psum(lax.dot_general(hot, hist, (((0,), (0,)), ((), ())), precision=l...  481 us
    gather x3, local copies, waits for them, and re-layouts, body(): rho_cell = whole[:, 0, :].reshape(-1)[index]  69.2 us
    gather x4, local copies, waits for them, and re-layouts, body(): temp_cell = whole[:, 1, :].reshape(-1)[index]  68.6 us
  transfers between devices with their start and end apart: 8, of which 6 were waited for; matrix products, arithmetic and copies ran while one was open for 0% of the time, Pallas kernels for 0%

commit v1 on v0

--- a/solution.py
+++ b/solution.py
@@ -95,7 +95,12 @@
             - 0.2 * jax.nn.sigmoid(cond[3]) * (temp - 0.5)
         )
         table = jnp.stack([rho_c, temp_c])[None]
-        whole = lax.all_gather(table, ("sec", "span"), axis=0, tiled=True)
+        whole = jnp.concatenate(
+            lax.all_to_all(
+                jnp.stack([table] * lax.axis_size(("sec", "span"))), ("sec", "span"), 0, 0
+            ),
+            axis=0,
+        )
         rho_cell = whole[:, 0, :].reshape(-1)[index]
         temp_cell = whole[:, 1, :].reshape(-1)[index]
         extended = extended_2(fields, (("span", 2),), 1)

time: 1920 us -> 730 us (0.38)
  blocking collectives: 1250 us -> 0 us
  waiting for transfers between devices: 490 us -> 518 us
  starting transfers between devices: 11.1 us -> 36.3 us
    all_gather x2 -> x0, blocking collectives: 1250 us -> none  [body(): whole = lax.all_gather(table, ('sec', 'span'), axis=0, tiled=True)]
    all_to_all x0 -> x2, starting transfers between devices: none -> 22.8 us  [body(): lax.all_to_all(jnp.stack([table] * lax.axis_size(('sec', 'span'))), ('sec...]
  transfers between devices with their start and end apart: 8 -> 10, of which waited for: 6 -> 6; matrix products, arithmetic and copies ran while one was open for 0% -> 1% of each run, Pallas kernels for 0% -> 0%
where the time goes in v1:
time: 730 us; the launch traced here: 726 us
  waiting for transfers between devices  518 us (71%)
  local copies, waits for them, and re-layouts  146 us (20%)
  starting transfers between devices  36.3 us (5%)
  between operations  14.4 us (2%)
  matrix products  7.84 us (1%)
    psum x2, waiting for transfers between devices, body(): lax.psum(lax.dot_general(hot, hist, (((0,), (0,)), ((), ())), precision=l...  494 us
    gather x3, local copies, waits for them, and re-layouts, body(): rho_cell = whole[:, 0, :].reshape(-1)[index]  69.2 us
    gather x4, local copies, waits for them, and re-layouts, body(): temp_cell = whole[:, 1, :].reshape(-1)[index]  68.6 us
    all_to_all x2, starting transfers between devices, body(): lax.all_to_all(jnp.stack([table] * lax.axis_size(('sec', 'span'))), ('sec...  22.8 us
    all_to_all x2, waiting for transfers between devices, body(): lax.all_to_all(jnp.stack([table] * lax.axis_size(('sec', 'span'))), ('sec...  17.8 us
  transfers between devices with their start and end apart: 10, of which 6 were waited for; matrix products, arithmetic and copies ran while one was open for 1% of the time, Pallas kernels for 0%

profile of v1, /device:TPU:0, one launch (start us, length us, event | category | flops | bytes accessed | tf_op | source)
XLA Modules:
  0.0 726.4 jit_solution(18070996482716206167)
XLA Ops:
  7.2 0.8 stack.44
  8.1 0.8 bitcast_multiply_fusion
  10.0 2.4 while.22
  10.0 0.8 fusion.68
  10.8 0.8 fusion.68
  11.6 0.8 fusion.68
  13.1 1.4 fusion.21
  15.2 1.8 collective-permute-start
  17.0 5.3 collective-permute-start.1
  22.4 248.3 %all-reduce.5.cloned.1.call-done = f32[256,640]{1,0:T(8,128)} async-done(((f32[256,640]{1,0:T(8,128)}), f32[256,640]{1,0:T(8,128)}) %all-reduce.5.cloned.1.call-update) | async-done | bytes 655376 | tf_op jit(solution)/shard_map/psum | solution.py:55
  271.4 0.8 dynamic-slice.16
  273.1 0.8 stack.51
  273.9 11.4 %all-to-all-start = ((f32[256,1,2,128]{3,2,1,0:T(2,128)}), f32[256,1,2,128]{3,2,1,0:T(2,128)S(1)}, u32[]{:S(2)}, u32[]{:S(2)}) async-start(f32[256,1,2,128]{3,2,1,0:T(2,128)} %stack.51), calls=%async_computation | async-start | bytes 524288 | tf_op jit(solution)/shard_map/all_to_all | solution.py:99
  285.6 13.9 %all-to-all-done = f32[256,1,2,128]{3,2,1,0:T(2,128)S(1)} async-done(((f32[256,1,2,128]{3,2,1,0:T(2,128)}), f32[256,1,2,128]{3,2,1,0:T(2,128)S(1)}, u32[]{:S(2)}, u32[]{:S(2)}) %all-to-all-start) | async-done | bytes 262176 | tf_op jit(solution)/shard_map/all_to_all | solution.py:99
  299.8 34.3 %gather_fusion.1 = f32[6144]{0:T(1024)S(1)} fusion(f32[32768]{0:T(1024)S(1)} %bitcast.130, s32[6144]{0:T(1024)S(1)} %broadcast_clamp_fusion), kind=kCustom, calls=%fused_computation.1 | custom fusion | bytes 73728 | tf_op jit(solution)/shard_map/gather | solution.py:105
  334.1 34.3 %gather_fusion = f32[6144]{0:T(1024)S(1)} fusion(f32[32768]{0:T(1024)S(1)} %bitcast.128, s32[6144]{0:T(1024)S(1)} %broadcast_clamp_fusion), kind=kCustom, calls=%fused_computation | custom fusion | bytes 73728 | tf_op jit(solution)/shard_map/gather | solution.py:104
  368.7 2.5 while.23
  368.8 0.8 fusion.70
  369.6 0.8 fusion.70
  370.4 0.8 fusion.70
  371.2 1.4 fusion.18
  372.6 2.5 collective-permute-start.3
  375.2 245.5 %all-reduce.7.cloned.1.call-done = f32[256,640]{1,0:T(8,128)} async-done(((f32[256,640]{1,0:T(8,128)}), f32[256,640]{1,0:T(8,128)}) %all-reduce.7.cloned.1.call-update) | async-done | bytes 655376 | tf_op jit(solution)/shard_map/psum | solution.py:55
  621.3 0.8 dynamic-slice.18
  623.0 0.8 stack.55
  623.8 11.4 %all-to-all-start.1 = ((f32[256,1,2,128]{3,2,1,0:T(2,128)}), f32[256,1,2,128]{3,2,1,0:T(2,128)S(1)}, u32[]{:S(2)}, u32[]{:S(2)}) async-start(f32[256,1,2,128]{3,2,1,0:T(2,128)} %stack.55), calls=%async_computation.1 | async-start | bytes 524288 | tf_op jit(solution)/shard_map/all_to_all | solution.py:99
  635.3 3.8 collective-permute-start.4
  639.1 1.7 collective-permute-done.4
  640.9 4.6 collective-permute-done.5
  645.6 3.9 all-to-all-done.1
  649.7 34.3 %gather_fusion.3 = f32[6144]{0:T(1024)S(1)} fusion(f32[32768]{0:T(1024)S(1)} %bitcast.131, s32[6144]{0:T(1024)S(1)} %broadcast_clamp_fusion), kind=kCustom, calls=%fused_computation.3 | custom fusion | bytes 73728 | tf_op jit(solution)/shard_map/gather | solution.py:105
  684.0 34.3 %gather_fusion.2 = f32[6144]{0:T(1024)S(1)} fusion(f32[32768]{0:T(1024)S(1)} %bitcast.129, s32[6144]{0:T(1024)S(1)} %broadcast_clamp_fusion), kind=kCustom, calls=%fused_computation.2 | custom fusion | bytes 73728 | tf_op jit(solution)/shard_map/gather | solution.py:104
  (72 shorter events, 8.2 us)
Async XLA Ops:
  7.2 265.1 %copy-start = (f32[32,32]{1,0:T(8,128)S(1)}, f32[32,32]{1,0:T(8,128)}, u32[]{:S(2)}) copy-start(f32[32,32]{1,0:T(8,128)} %param.21) | copy-start | bytes 12292
  7.2 263.5 %all-reduce.5.cloned.1.call-start = ((), (), s32[]{:S(2)}) async-start(), calls=%async_computation.2 | async-start | bytes 1310720 | tf_op jit(solution)/shard_map/psum | solution.py:55
  7.2 0.8 copy-start.4
  9.2 0.7 copy-start.2
  12.4 0.7 copy-start.5
  14.5 0.7 copy-start.7
  14.5 2.5 copy-start.1
  15.2 257.0 %collective-permute-start = (f32[1,32,128]{2,1,0:T(8,128)S(1)}, f32[1,32,128]{2,1,0:T(8,128)S(1)}, u32[]{:S(2)}, u32[]{:S(2)}) collective-permute-start(f32[1,32,128]{2,1,0:T(8,128)S(1)} %copy-done.7), channel_id=1, source_target_pairs={{0,1},{1,2},{2,3},{3,4},{4,5},{5,6},{6,7},{7,8},{8,9},{9,10},{10,1... | collective-permute-start | bytes 49160 | tf_op jit(solution)/shard_map/ppermute | solution.py:13
  17.0 268.4 %collective-permute-start.1 = (f32[4,24,1]{2,1,0:T(8,128)S(1)}, f32[4,24,1]{2,1,0:T(8,128)S(1)}, u32[]{:S(2)}, u32[]{:S(2)}) collective-permute-start(f32[4,24,1]{2,1,0:T(8,128)S(1)} %get-tuple-element.108), channel_id=1, source_target_pairs={{1,0},{2,1},{3,2},{4,3},{5,4},{6,5},{7,6},{8,7},{9,8},{10,9},{11,1... | collective-permute-start | bytes 1160 | tf_op jit(solution)/shard_map/ppermute | solution.py:24
  22.4 263.1 %collective-permute-start.2 = (f32[4,24,1]{2,1,0:T(8,128)S(1)}, f32[4,24,1]{2,1,0:T(8,128)S(1)}, u32[]{:S(2)}, u32[]{:S(2)}) collective-permute-start(f32[4,24,1]{2,1,0:T(8,128)S(1)} %get-tuple-element.109), channel_id=1, source_target_pairs={{0,1},{1,2},{2,3},{3,4},{4,5},{5,6},{6,7},{7,8},{8,9},{9,10},{10,1... | collective-permute-start | bytes 1160 | tf_op jit(solution)/shard_map/ppermute | solution.py:23
  272.2 0.7 copy-start.6
  272.2 0.7 copy-start.8
  273.9 25.7 %all-to-all-start = ((f32[256,1,2,128]{3,2,1,0:T(2,128)}), f32[256,1,2,128]{3,2,1,0:T(2,128)S(1)}, u32[]{:S(2)}, u32[]{:S(2)}) async-start(f32[256,1,2,128]{3,2,1,0:T(2,128)} %stack.51), calls=%async_computation | async-start | bytes 524288 | tf_op jit(solution)/shard_map/all_to_all | solution.py:99
  285.3 335.3 %all-reduce.7.cloned.1.call-start = ((), (), s32[]{:S(2)}) async-start(), calls=%async_computation.3 | async-start | bytes 1310720 | tf_op jit(solution)/shard_map/psum | solution.py:55
  372.6 249.7 %collective-permute-start.3 = (f32[1,32,128]{2,1,0:T(8,128)S(1)}, f32[1,32,128]{2,1,0:T(8,128)S(1)}, u32[]{:S(2)}, u32[]{:S(2)}) collective-permute-start(f32[1,32,128]{2,1,0:T(8,128)S(1)} %bitcast.139), channel_id=1, source_target_pairs={{0,1},{1,2},{2,3},{3,4},{4,5},{5,6},{6,7},{7,8},{8,9},{9,10},{10,1... | collective-permute-start | bytes 49160 | tf_op jit(solution)/shard_map/ppermute | solution.py:13
  623.8 25.7 %all-to-all-start.1 = ((f32[256,1,2,128]{3,2,1,0:T(2,128)}), f32[256,1,2,128]{3,2,1,0:T(2,128)S(1)}, u32[]{:S(2)}, u32[]{:S(2)}) async-start(f32[256,1,2,128]{3,2,1,0:T(2,128)} %stack.55), calls=%async_computation.1 | async-start | bytes 524288 | tf_op jit(solution)/shard_map/all_to_all | solution.py:99
  635.3 5.6 collective-permute-start.4
  639.1 6.4 collective-permute-start.5
  718.9 0.6 copy-start.3
Sparse Core Ops, SparseCore 0:
  14.6 256.0 all-reduce.4
  372.8 247.8 all-reduce.6
